TPU v7x, 32 devices: a whole 2x2x4 slice. The times are simulated.
32 devices in a mesh: grp: 2 (over y), rows: 8 (over z, x), mod: 2 (over core).
Axes of the slice: x: 2, y: 2, z: 4, core: 2. Of those that a mesh axis runs over, the one named last changes fastest.
Arguments:
- queries: bfloat16 [16, 8, 2304], P(('grp', 'rows'), 'mod'), parts along dimension 0, may hold values from -6 to 6
- train_grads: bfloat16 [2048, 8, 2304], P(('grp', 'rows'), 'mod'), parts along dimension 0, may hold values from -6 to 6
- factors: float32 [8, 2, 48, 48], P('mod'), may hold values from -4 to 4, as said below
Outputs:
- scores: float32 [16, 1024], P(('grp', 'mod'), 'rows'), parts along dimension 0
There are 2 independent parts, one for each index of `grp`. A program takes and returns all parts, laid end to end along the dimension named above; an argument that names none is the same for every part. Nothing has to cross between parts.
Inputs may be any that keep to these rules, and one draw needn't show every extreme that they name: `factors`: each factor is a 48 x 48 matrix with a positive diagonal and full rank.
All inputs are finite; a program needn't handle non-finite values.
Results may differ from a plain program's by a relative error of at most 0.0029.
Values may be sent and summed in bfloat16 or wider, within the bound.
No kernel may reach another device: no remote copies, remote signals or barrier semaphores. Data moves between devices by JAX's collectives and lax.ppermute only.
A program may use at most 64 MiB of HBM per device.

v0:
```python
import jax
import jax.numpy as jnp
from jax import lax
from jax.sharding import PartitionSpec as P

MODULES = 8
PROJ = 48
COORDS = 2304


def precondition(grads_in, factors):
    count = grads_in.shape[0]
    local_modules = grads_in.shape[1]
    grads = grads_in.astype(jnp.float32).reshape(count, local_modules, PROJ, PROJ)
    left_side = jnp.einsum("mab,qmbc->qmac", factors[:, 0], grads, precision=lax.Precision.HIGHEST)
    both_sides = jnp.einsum(
        "qmac,mcd->qmad", left_side, factors[:, 1], precision=lax.Precision.HIGHEST
    )
    both_sides = both_sides / jnp.sqrt(jnp.float32(MODULES * COORDS))
    return both_sides.astype(jnp.bfloat16).reshape(count, local_modules, PROJ * PROJ)


def shards(queries, train_grads, factors):
    train_count = train_grads.shape[0]
    train_flat = train_grads.reshape(train_count, -1)
    scaled_own = precondition(queries, factors)
    ready_rows = lax.all_gather(scaled_own, "rows", axis=0, tiled=True)
    flat_rows = ready_rows.reshape(ready_rows.shape[0], -1)
    partial_value = lax.dot_general(
        flat_rows, train_flat, (((1,), (1,)), ((), ())), preferred_element_type=jnp.float32
    )
    return lax.psum_scatter(partial_value, "mod", scatter_dimension=0, tiled=True)


def solution(mesh):
    in_specs = (
        P(("grp", "rows"), "mod", None),
        P(("grp", "rows"), "mod", None),
        P("mod", None, None, None),
    )
    out_specs = P(("grp", "mod"), "rows")
    return jax.shard_map(shards, mesh=mesh, in_specs=in_specs, out_specs=out_specs, check_vma=False)
```

profile of v0, /device:TPU:0, one launch (start us, length us, event | category | flops | bytes accessed | tf_op | source)
XLA Modules:
  0.0 40.9 jit_solution(16463728505834022918)
XLA Ops:
  0.0 0.0 copy-start
  0.0 0.0 copy-start.1
  0.0 1.0 %reshape.18 = bf16[4,48,48]{2,1,0:T(8,128)(2,1)S(1)} reshape(bf16[1,4,2304]{2,1,0:T(4,128)(2,1)} %param.3) | data formatting | bytes 36864 | tf_op jit(solution)/shard_map/reshape
  1.0 1.2 %convolution_bitcast_fusion = f32[4,48,48]{1,2,0:T(8,128)S(1)} fusion(bf16[4,48,48]{2,1,0:T(8,128)(2,1)S(1)} %reshape.18, f32[4,2,48,48]{3,2,1,0:T(8,128)} %param.5), kind=kOutput, calls=%fused_computation.3 | convolution fusion | flops 5308416 | bytes 153600 | tf_op jit(solution)/shard_map/mab,qmbc->qmac/dot_general | solution.py:15
  2.1 1.2 %fusion.3 = bf16[1,4,48,48]{3,2,1,0:T(8,128)(2,1)S(1)} fusion(f32[4,48,48]{1,2,0:T(8,128)S(1)} %convolution_bitcast_fusion, f32[4,2,48,48]{3,2,1,0:T(8,128)} %param.5), kind=kOutput, calls=%fused_computation.5 | convolution fusion | flops 5326848 | bytes 153600 | tf_op jit(solution)/shard_map/qmac,mcd->qmad/dot_general | solution.py:16
  3.4 0.1 reshape.20
  3.5 32.4 %all_gather.3 = bf16[8,4,2304]{2,1,0:T(4,128)(2,1)S(1)} all-gather(bf16[1,4,2304]{2,1,0:T(4,128)(2,1)S(1)} %reshape.20), channel_id=1, replica_groups=mesh['grp'=2,'rows'=8,'mod'=2] {'rows'}, dimensions={0}, use_global_device_ids=true | all-gather | bytes 165888 | tf_op jit(solution)/shard_map/all_gather | solution.py:27
  35.9 0.0 copy-done
  35.9 0.7 %fusion.4 = f32[8,128]{1,0:T(8,128)S(1)} fusion(bf16[128,4,2304]{2,1,0:T(4,128)(2,1)S(1)} %copy-done, bf16[8,4,2304]{2,1,0:T(4,128)(2,1)S(1)} %all_gather.3), kind=kOutput, calls=%fused_computation.6 | convolution fusion | flops 18874368 | bytes 2510848 | tf_op jit(solution)/shard_map/dot_general | solution.py:29
  36.6 2.5 %all-reduce = f32[8,128]{1,0:T(8,128)S(1)} all-reduce(f32[8,128]{1,0:T(8,128)S(1)} %fusion.4), channel_id=2, replica_groups=mesh['grp'=2,'rows'=8,'mod'=2] {'mod'}, use_global_device_ids=true, to_apply=%region_0.0.clone | all-reduce | flops 1024 | bytes 8192
  39.1 0.0 copy-done.1
  39.1 0.6 %dynamic-slice = u32[1]{0:T(128)} dynamic-slice(u32[32]{0:T(128)S(1)} %copy-done.1, u32[]{:T(128)S(6)} %add.3), dynamic_slice_sizes={1} | dynamic-slice | bytes 12
  40.3 0.6 %constant_dynamic-slice_fusion = f32[4,128]{1,0:T(4,128)} fusion(f32[8,128]{1,0:T(8,128)S(1)} %all-reduce, u32[]{:T(128)S(6)} %multiply.5), kind=kLoop, calls=%fused_computation.12 | loop fusion | bytes 4100
Async XLA Ops:
  0.0 35.9 %copy-start = (bf16[128,4,2304]{2,1,0:T(4,128)(2,1)S(1)}, bf16[128,4,2304]{2,1,0:T(4,128)(2,1)}, u32[]{:S(2)}) copy-start(bf16[128,4,2304]{2,1,0:T(4,128)(2,1)} %param.4) | copy-start | bytes 7077892
  0.0 39.1 %copy-start.1 = (u32[32]{0:T(128)S(1)}, u32[32]{0:T(128)}, u32[]{:S(2)}) copy-start(u32[32]{0:T(128)} %constant.6) | copy-start | bytes 388
where the time goes:
time: 41.1 us; the launch traced here: 40.9 us
  blocking collectives  34.8 us (85%)
  matrix products  3.1 us (8%)
  local copies, waits for them, and re-layouts  2.27 us (6%)
  between operations  0.68 us (2%)
    all_gather x1, blocking collectives, shards(): ready_rows = lax.all_gather(scaled_own, 'rows', axis=0, tiled=True)  32.4 us
    unnamed x1, blocking collectives  2.46 us
    dot_general x1, matrix products, precondition(): jnp.einsum('qmac,mcd->qmad', left_side, factors[:, 1], precision=lax.Prec...  1.24 us
    unnamed x6, local copies, waits for them, and re-layouts  1.18 us
    dot_general x1, matrix products, precondition(): jnp.einsum('mab,qmbc->qmac', factors[:, 0], grads, precision=lax.Precisio...  1.15 us
    reshape x1, local copies, waits for them, and re-layouts  0.98 us

commit v1 on v0

--- a/solution.py
+++ b/solution.py
@@ -6,6 +6,12 @@
 MODULES = 8
 PROJ = 48
 COORDS = 2304
+
+
+def joined_along(pieces, dim):
+    pieces = jnp.moveaxis(pieces, 0, dim)
+    dims = pieces.shape
+    return pieces.reshape(*dims[:dim], dims[dim] * dims[dim + 1], *dims[dim + 2 :])
 
 
 def precondition(grads_in, factors):
@@ -24,7 +30,19 @@
     train_count = train_grads.shape[0]
     train_flat = train_grads.reshape(train_count, -1)
     scaled_own = precondition(queries, factors)
-    ready_rows = lax.all_gather(scaled_own, "rows", axis=0, tiled=True)
+    size = lax.axis_size("rows")
+    pairs = [(i, (i + 1) % size) for i in range(size)]
+    back = [(b, a) for a, b in pairs]
+    lower, upper = ([], [])
+    for step in range(size - 1):
+        if step % 2 == 0:
+            lower.append(lax.ppermute(lower[-1] if lower else scaled_own, "rows", pairs))
+        else:
+            upper.append(lax.ppermute(upper[-1] if upper else scaled_own, "rows", back))
+    tiles = jnp.stack([*lower[::-1], scaled_own, *upper])
+    shift = lax.axis_index("rows") - len(lower)
+    tiles = tiles[(jnp.arange(size) - shift) % size]
+    ready_rows = joined_along(tiles, 0)
     flat_rows = ready_rows.reshape(ready_rows.shape[0], -1)
     partial_value = lax.dot_general(
         flat_rows, train_flat, (((1,), (1,)), ((), ())), preferred_element_type=jnp.float32

time: 41.1 us -> 38.5 us (0.937)
  blocking collectives: 34.8 us -> 2.47 us
  starting transfers between devices: 0 us -> 17.3 us
  waiting for transfers between devices: 0 us -> 9.5 us
  local copies, waits for them, and re-layouts: 2.27 us -> 5.02 us
    all_gather x1 -> x0, blocking collectives: 32.4 us -> none  [shards(): ready_rows = lax.all_gather(scaled_own, 'rows', axis=0, tiled=True)]
    ppermute x0 -> x7, starting transfers between devices: none -> 17.3 us  [the longest x3 14.3 us: shards(): upper.append(lax.ppermute(upper[-1] if upper else scaled_own, 'rows', back))]
    ppermute x0 -> x7, waiting for transfers between devices: none -> 9.5 us  [the longest x4 8.18 us: shards(): lax.ppermute(lower[-1] if lower else scaled_own, 'rows', pairs)]
    unnamed x6 -> x13, local copies, waits for them, and re-layouts: 1.18 us -> 3.27 us
    gather x0 -> x1, local copies, waits for them, and re-layouts: none -> 0.67 us  [shards(): tiles = tiles[(jnp.arange(size) - shift) % size]]
  transfers between devices with their start and end apart: 0 -> 7, of which waited for: 0 -> 4; matrix products, arithmetic and copies ran while one was open for 0% -> 7% of each run, Pallas kernels for 0% -> 0%
where the time goes in v1:
time: 38.5 us; the launch traced here: 38.2 us
  starting transfers between devices  17.3 us (45%)
  waiting for transfers between devices  9.5 us (25%)
  local copies, waits for them, and re-layouts  5.02 us (13%)
  matrix products  3.09 us (8%)
  blocking collectives  2.47 us (6%)
  between operations  0.8 us (2%)
    ppermute x3, starting transfers between devices, shards(): upper.append(lax.ppermute(upper[-1] if upper else scaled_own, 'rows', back))  14.3 us
    ppermute x4, waiting for transfers between devices, shards(): lax.ppermute(lower[-1] if lower else scaled_own, 'rows', pairs)  8.18 us
    unnamed x13, local copies, waits for them, and re-layouts  3.27 us
    ppermute x4, starting transfers between devices, shards(): lax.ppermute(lower[-1] if lower else scaled_own, 'rows', pairs)  3.03 us
    unnamed x1, blocking collectives  2.47 us
    ppermute x3, waiting for transfers between devices, shards(): upper.append(lax.ppermute(upper[-1] if upper else scaled_own, 'rows', back))  1.32 us
    dot_general x1, matrix products, precondition(): jnp.einsum('qmac,mcd->qmad', left_side, factors[:, 1], precision=lax.Prec...  1.24 us
    dot_general x1, matrix products, precondition(): jnp.einsum('mab,qmbc->qmac', factors[:, 0], grads, precision=lax.Precisio...  1.15 us
  transfers between devices with their start and end apart: 7, of which 4 were waited for; matrix products, arithmetic and copies ran while one was open for 7% of the time, Pallas kernels for 0%

profile of v1, /device:TPU:0, one launch (start us, length us, event | category | flops | bytes accessed | tf_op | source)
XLA Modules:
  0.0 38.2 jit_solution(17174488440000834090)
XLA Ops:
  0.0 0.8 %reshape.68 = bf16[4,48,48]{2,1,0:T(8,128)(2,1)S(1)} reshape(bf16[1,4,2304]{2,1,0:T(4,128)(2,1)} %param.3) | data formatting | bytes 36864 | tf_op jit(solution)/shard_map/reshape
  0.8 1.2 %convolution_bitcast_fusion = f32[4,48,48]{1,2,0:T(8,128)S(1)} fusion(bf16[4,48,48]{2,1,0:T(8,128)(2,1)S(1)} %reshape.68, f32[4,2,48,48]{3,2,1,0:T(8,128)} %param.5), kind=kOutput, calls=%fused_computation.2 | convolution fusion | flops 5308416 | bytes 153600 | tf_op jit(solution)/shard_map/mab,qmbc->qmac/dot_general | solution.py:21
  2.0 1.2 %fusion.1 = bf16[1,4,48,48]{3,2,1,0:T(8,128)(2,1)S(1)} fusion(f32[4,48,48]{1,2,0:T(8,128)S(1)} %convolution_bitcast_fusion, f32[4,2,48,48]{3,2,1,0:T(8,128)} %param.5), kind=kOutput, calls=%fused_computation.4 | convolution fusion | flops 5326848 | bytes 153600 | tf_op jit(solution)/shard_map/qmac,mcd->qmad/dot_general | solution.py:22
  3.2 0.1 reshape.70
  3.4 3.0 %collective-permute-start = (bf16[1,4,2304]{2,1,0:T(4,128)(2,1)S(1)}, bf16[1,4,2304]{2,1,0:T(4,128)(2,1)S(1)}, u32[]{:S(2)}, u32[]{:S(2)}) collective-permute-start(bf16[1,4,2304]{2,1,0:T(4,128)(2,1)S(1)} %reshape.70), channel_id=1, source_target_pairs={{0,2},{2,4},{4,6},{6,8},{8,10},{10,12},{12,14},{14,0},{1,3},{3,5},... | collective-permute-start | bytes 55304 | tf_op jit(solution)/shard_map/ppermute | solution.py:39
  6.4 4.8 %collective-permute-done = bf16[1,4,2304]{2,1,0:T(4,128)(2,1)S(1)} collective-permute-done((bf16[1,4,2304]{2,1,0:T(4,128)(2,1)S(1)}, bf16[1,4,2304]{2,1,0:T(4,128)(2,1)S(1)}, u32[]{:S(2)}, u32[]{:S(2)}) %collective-permute-start) | collective-permute-done | bytes 18464 | tf_op jit(solution)/shard_map/ppermute | solution.py:39
  11.2 0.0 collective-permute-start.1
  11.2 4.7 %collective-permute-start.4 = (bf16[1,4,2304]{2,1,0:T(4,128)(2,1)S(1)}, bf16[1,4,2304]{2,1,0:T(4,128)(2,1)S(1)}, u32[]{:S(2)}, u32[]{:S(2)}) collective-permute-start(bf16[1,4,2304]{2,1,0:T(4,128)(2,1)S(1)} %reshape.70), channel_id=1, source_target_pairs={{2,0},{4,2},{6,4},{8,6},{10,8},{12,10},{14,12},{0,14},{3,1},{5,3},... | collective-permute-start | bytes 55304 | tf_op jit(solution)/shard_map/ppermute | solution.py:41
  15.9 1.7 %collective-permute-done.1 = bf16[1,4,2304]{2,1,0:T(4,128)(2,1)S(1)} collective-permute-done((bf16[1,4,2304]{2,1,0:T(4,128)(2,1)S(1)}, bf16[1,4,2304]{2,1,0:T(4,128)(2,1)S(1)}, u32[]{:S(2)}, u32[]{:S(2)}) %collective-permute-start.1) | collective-permute-done | bytes 18464 | tf_op jit(solution)/shard_map/ppermute | solution.py:39
  17.6 0.0 collective-permute-start.2
  17.6 0.0 collective-permute-done.4
  17.6 4.8 %collective-permute-start.5 = (bf16[1,4,2304]{2,1,0:T(4,128)(2,1)S(1)}, bf16[1,4,2304]{2,1,0:T(4,128)(2,1)S(1)}, u32[]{:S(2)}, u32[]{:S(2)}) collective-permute-start(bf16[1,4,2304]{2,1,0:T(4,128)(2,1)S(1)} %collective-permute-done.4), channel_id=1, source_target_pairs={{2,0},{4,2},{6,4},{8,6},{10,8},{12,10},{14,12},{0,14},{3,1},{5,3},... | collective-permute-start | bytes 55304 | tf_op jit(solution)/shard_map/ppermute | solution.py:41
  22.4 1.7 %collective-permute-done.2 = bf16[1,4,2304]{2,1,0:T(4,128)(2,1)S(1)} collective-permute-done((bf16[1,4,2304]{2,1,0:T(4,128)(2,1)S(1)}, bf16[1,4,2304]{2,1,0:T(4,128)(2,1)S(1)}, u32[]{:S(2)}, u32[]{:S(2)}) %collective-permute-start.2) | collective-permute-done | bytes 18464 | tf_op jit(solution)/shard_map/ppermute | solution.py:39
  24.1 0.0 collective-permute-start.3
  24.1 0.1 stack_reshape.3
  24.2 0.0 copy-start
  24.2 2.0 %copy.17 = bf16[16,8,4,2304]{3,1,2,0:T(8,128)(2,1)S(1)} copy(bf16[16,8,4,2304]{3,2,1,0:T(4,128)(2,1)} %bitcast.53) | data formatting | bytes 4718592
  26.2 0.0 copy-done
  26.2 0.6 %dynamic-slice = u32[1]{0:T(128)} dynamic-slice(u32[32]{0:T(128)S(1)} %copy-done, u32[]{:T(128)S(6)} %add.29), dynamic_slice_sizes={1} | dynamic-slice | bytes 12
  27.5 0.0 collective-permute-done.5
  27.5 4.8 %collective-permute-start.6 = (bf16[1,4,2304]{2,1,0:T(4,128)(2,1)S(1)}, bf16[1,4,2304]{2,1,0:T(4,128)(2,1)S(1)}, u32[]{:S(2)}, u32[]{:S(2)}) collective-permute-start(bf16[1,4,2304]{2,1,0:T(4,128)(2,1)S(1)} %collective-permute-done.5), channel_id=1, source_target_pairs={{2,0},{4,2},{6,4},{8,6},{10,8},{12,10},{14,12},{0,14},{3,1},{5,3},... | collective-permute-start | bytes 55304 | tf_op jit(solution)/shard_map/ppermute | solution.py:41
  32.2 0.0 collective-permute-done.3
  32.4 1.3 %collective-permute-done.6 = bf16[1,4,2304]{2,1,0:T(4,128)(2,1)S(1)} collective-permute-done((bf16[1,4,2304]{2,1,0:T(4,128)(2,1)S(1)}, bf16[1,4,2304]{2,1,0:T(4,128)(2,1)S(1)}, u32[]{:S(2)}, u32[]{:S(2)}) %collective-permute-start.6) | collective-permute-done | bytes 18464 | tf_op jit(solution)/shard_map/ppermute | solution.py:41
  33.7 0.7 %gather_fusion = bf16[8,4,2304]{2,1,0:T(4,128)(2,1)S(1)} fusion(bf16[8,4,2304]{2,1,0:T(4,128)(2,1)S(1)} %bitcast.56, s32[1024]{0:T(1024)S(1)} %pad_clamp_fusion), kind=kCustom, calls=%fused_computation | custom fusion | bytes 294944 | tf_op jit(solution)/shard_map/gather | solution.py:44
  34.4 0.7 %fusion.8 = f32[8,128]{1,0:T(8,128)S(1)} fusion(bf16[8,9216]{1,0:T(8,128)(2,1)S(1)} %bitcast.54, bf16[128,9216]{1,0:T(8,128)(2,1)S(1)} %bitcast.52), kind=kOutput, calls=%fused_computation.25 | convolution fusion | flops 18874368 | bytes 2510848 | tf_op jit(solution)/shard_map/dot_general | solution.py:47
  35.1 2.5 %all-reduce = f32[8,128]{1,0:T(8,128)S(1)} all-reduce(f32[8,128]{1,0:T(8,128)S(1)} %fusion.8), channel_id=2, replica_groups=mesh['grp'=2,'rows'=8,'mod'=2] {'mod'}, use_global_device_ids=true, to_apply=%region_0.1.clone | all-reduce | flops 1024 | bytes 8192
  37.6 0.6 %constant_dynamic-slice_fusion = f32[4,128]{1,0:T(4,128)} fusion(f32[8,128]{1,0:T(8,128)S(1)} %all-reduce, u32[]{:T(128)S(6)} %multiply.5), kind=kLoop, calls=%fused_computation.24 | loop fusion | bytes 4100
  (11 shorter events, 0.2 us)
Async XLA Ops:
  3.4 7.8 %collective-permute-start = (bf16[1,4,2304]{2,1,0:T(4,128)(2,1)S(1)}, bf16[1,4,2304]{2,1,0:T(4,128)(2,1)S(1)}, u32[]{:S(2)}, u32[]{:S(2)}) collective-permute-start(bf16[1,4,2304]{2,1,0:T(4,128)(2,1)S(1)} %reshape.70), channel_id=1, source_target_pairs={{0,2},{2,4},{4,6},{6,8},{8,10},{10,12},{12,14},{14,0},{1,3},{3,5},... | collective-permute-start | bytes 55304 | tf_op jit(solution)/shard_map/ppermute | solution.py:39
  11.2 6.5 %collective-permute-start.1 = (bf16[1,4,2304]{2,1,0:T(4,128)(2,1)S(1)}, bf16[1,4,2304]{2,1,0:T(4,128)(2,1)S(1)}, u32[]{:S(2)}, u32[]{:S(2)}) collective-permute-start(bf16[1,4,2304]{2,1,0:T(4,128)(2,1)S(1)} %collective-permute-done), channel_id=1, source_target_pairs={{0,2},{2,4},{4,6},{6,8},{8,10},{10,12},{12,14},{14,0},{1,3},{3,5},... | collective-permute-start | bytes 55304 | tf_op jit(solution)/shard_map/ppermute | solution.py:39
  11.2 6.5 %collective-permute-start.4 = (bf16[1,4,2304]{2,1,0:T(4,128)(2,1)S(1)}, bf16[1,4,2304]{2,1,0:T(4,128)(2,1)S(1)}, u32[]{:S(2)}, u32[]{:S(2)}) collective-permute-start(bf16[1,4,2304]{2,1,0:T(4,128)(2,1)S(1)} %reshape.70), channel_id=1, source_target_pairs={{2,0},{4,2},{6,4},{8,6},{10,8},{12,10},{14,12},{0,14},{3,1},{5,3},... | collective-permute-start | bytes 55304 | tf_op jit(solution)/shard_map/ppermute | solution.py:41
  17.6 6.5 %collective-permute-start.2 = (bf16[1,4,2304]{2,1,0:T(4,128)(2,1)S(1)}, bf16[1,4,2304]{2,1,0:T(4,128)(2,1)S(1)}, u32[]{:S(2)}, u32[]{:S(2)}) collective-permute-start(bf16[1,4,2304]{2,1,0:T(4,128)(2,1)S(1)} %collective-permute-done.1), channel_id=1, source_target_pairs={{0,2},{2,4},{4,6},{6,8},{8,10},{10,12},{12,14},{14,0},{1,3},{3,5},... | collective-permute-start | bytes 55304 | tf_op jit(solution)/shard_map/ppermute | solution.py:39
  17.6 9.8 %collective-permute-start.5 = (bf16[1,4,2304]{2,1,0:T(4,128)(2,1)S(1)}, bf16[1,4,2304]{2,1,0:T(4,128)(2,1)S(1)}, u32[]{:S(2)}, u32[]{:S(2)}) collective-permute-start(bf16[1,4,2304]{2,1,0:T(4,128)(2,1)S(1)} %collective-permute-done.4), channel_id=1, source_target_pairs={{2,0},{4,2},{6,4},{8,6},{10,8},{12,10},{14,12},{0,14},{3,1},{5,3},... | collective-permute-start | bytes 55304 | tf_op jit(solution)/shard_map/ppermute | solution.py:41
  24.1 8.2 %collective-permute-start.3 = (bf16[1,4,2304]{2,1,0:T(4,128)(2,1)S(1)}, bf16[1,4,2304]{2,1,0:T(4,128)(2,1)S(1)}, u32[]{:S(2)}, u32[]{:S(2)}) collective-permute-start(bf16[1,4,2304]{2,1,0:T(4,128)(2,1)S(1)} %collective-permute-done.2), channel_id=1, source_target_pairs={{0,2},{2,4},{4,6},{6,8},{8,10},{10,12},{12,14},{14,0},{1,3},{3,5},... | collective-permute-start | bytes 55304 | tf_op jit(solution)/shard_map/ppermute | solution.py:39
  24.2 2.0 %copy-start = (u32[32]{0:T(128)S(1)}, u32[32]{0:T(128)}, u32[]{:S(2)}) copy-start(u32[32]{0:T(128)} %constant.32) | copy-start | bytes 388
  27.5 6.2 %collective-permute-start.6 = (bf16[1,4,2304]{2,1,0:T(4,128)(2,1)S(1)}, bf16[1,4,2304]{2,1,0:T(4,128)(2,1)S(1)}, u32[]{:S(2)}, u32[]{:S(2)}) collective-permute-start(bf16[1,4,2304]{2,1,0:T(4,128)(2,1)S(1)} %collective-permute-done.5), channel_id=1, source_target_pairs={{2,0},{4,2},{6,4},{8,6},{10,8},{12,10},{14,12},{0,14},{3,1},{5,3},... | collective-permute-start | bytes 55304 | tf_op jit(solution)/shard_map/ppermute | solution.py:41
